TPU v7x, 32 devices: a whole 2x2x4 slice. The times are simulated.
32 devices in a mesh: groups: 2 (over y), wide: 4 (over x, core), narrow: 4 (over z).
Axes of the slice: x: 2, y: 2, z: 4, core: 2. Of those that a mesh axis runs over, the one named last changes fastest.
Arguments:
- basis: bfloat16 [128, 64, 2, 512], P(('groups', 'wide'), 'narrow'), parts along dimension 0, may hold values from -0.25 to 0.25
- kappa: float32 [128, 64, 2], P(('groups', 'wide'), 'narrow'), parts along dimension 0, may hold values from 0.1 to 1
- velocity: float32 [3, 512], P(None, 'groups'), parts along dimension 1, may hold values from -2 to 2
- coefficients: float32 [512, 512], P('groups'), parts along dimension 0, may hold values from -6 to 6
- propagator: float32 [1024, 512], P('groups'), parts along dimension 0, may hold values from -0.25 to 0.25
Outputs:
- advanced: float32 [512, 512], P(('groups', 'wide', 'narrow')), parts along dimension 0
There are 2 independent parts, one for each index of `groups`. A program takes and returns all parts, laid end to end along the dimension named above; each array names one. Nothing has to cross between parts.
All inputs are finite; a program needn't handle non-finite values.
Results may differ from a plain program's by a relative error of at most 0.0056.
Values may be sent and summed in bfloat16 or wider, within the bound.
A program may use at most 64 MiB of HBM per device.

v0:
```python
import math

import jax
import jax.numpy as jnp
from jax import lax
from jax.sharding import PartitionSpec as P

ITERS = 2


step_size = 4.0


def padded_2(x, sides, width):
    for axis, dim in sides:
        devices, length = (lax.axis_size(axis), x.shape[dim])
        up = [(i, (i + 1) % devices) for i in range(devices - 1)]
        down = [(j, i) for i, j in up]
        last = lax.slice_in_dim(x, length - width, length, axis=dim)
        first = lax.slice_in_dim(x, 0, width, axis=dim)
        before = lax.ppermute(last, axis, up)
        after = lax.ppermute(first, axis, down)
        x = jnp.concatenate([before, x, after], axis=dim)
    return x


def forcing_of(padded, kappa, velocity):
    center = padded[1:-1, 1:-1, 1:-1].astype(jnp.float32)
    x_next = padded[2:, 1:-1, 1:-1].astype(jnp.float32)
    x_prev = padded[:-2, 1:-1, 1:-1].astype(jnp.float32)
    y_next = padded[1:-1, 2:, 1:-1].astype(jnp.float32)
    y_prev = padded[1:-1, :-2, 1:-1].astype(jnp.float32)
    z_next = padded[1:-1, 1:-1, 2:].astype(jnp.float32)
    z_prev = padded[1:-1, 1:-1, :-2].astype(jnp.float32)
    spread = x_next + x_prev + y_next + y_prev + z_next + z_prev - 6.0 * center
    carried = velocity[0] * (x_next * x_next - x_prev * x_prev)
    carried = carried + velocity[1] * (y_next * y_next - y_prev * y_prev)
    carried = carried + velocity[2] * (z_next * z_next - z_prev * z_prev)
    result = kappa[..., None] * spread - 0.25 * carried
    return result.astype(jnp.bfloat16)


def advance(state, summed, scale, propagator):
    update = state + step_size * (summed * scale)
    return update + jnp.dot(
        update, propagator.T, precision=lax.Precision.HIGHEST, preferred_element_type=jnp.float32
    )


def body(basis, kappa, velocity, coefficients, propagator):
    size_x, size_y, size_z, modes = basis.shape
    columns = coefficients.shape[0]
    devices = lax.axis_size("wide") * lax.axis_size("narrow")
    owned = columns // devices
    scale = 1.0 / math.sqrt(size_x * size_y * size_z * devices)
    first_row = lax.axis_index(("wide", "narrow")) * owned
    flat_basis = basis.reshape(size_x * size_y * size_z, modes)
    lift_x, lift_y = (size_x, size_y)

    def lift_piece(piece):
        made = lax.dot_general(
            flat_basis, piece, (((1,), (1,)), ((), ())), preferred_element_type=jnp.float32
        )
        return made.astype(jnp.bfloat16)

    state = lax.dynamic_slice_in_dim(coefficients, first_row, owned, 0)
    lifted = lift_piece(coefficients.astype(jnp.bfloat16))
    for step in range(ITERS):
        field = lifted.reshape(lift_x, lift_y, size_z, columns)
        padded = padded_2(field, (("wide", 0), ("narrow", 1)), 1)
        padded = jnp.pad(padded, ((0, 0), (0, 0), (1, 1), (0, 0)))
        forcing = forcing_of(padded, kappa, velocity).reshape(size_x * size_y * size_z, columns)
        partial_rows = lax.psum_scatter(
            lax.dot_general(
                forcing, flat_basis, (((0,), (0,)), ((), ())), preferred_element_type=jnp.float32
            ),
            "wide",
            scatter_dimension=0,
            tiled=True,
        )
        summed = lax.psum_scatter(partial_rows, "narrow", scatter_dimension=0, tiled=True)
        state = advance(state, summed, scale, propagator)
        if step + 1 < ITERS:
            lifted = lift_piece(
                lax.all_gather(state.astype(jnp.bfloat16), ("wide", "narrow"), axis=0, tiled=True)
            )
    return state


def solution(mesh):
    placed = (
        P(("groups", "wide"), "narrow", None, None),
        P(("groups", "wide"), "narrow", None),
        P(None, "groups"),
        P("groups", None),
        P("groups", None),
    )
    return jax.shard_map(
        body,
        mesh=mesh,
        in_specs=placed,
        out_specs=P(("groups", "wide", "narrow"), None),
        check_vma=False,
    )
```

profile of v0, /device:TPU:0, one launch (start us, length us, event | category | flops | bytes accessed | tf_op | source)
XLA Modules:
  0.0 175.8 jit_solution(13818191396235524787)
XLA Ops:
  6.5 0.0 copy-start
  6.5 0.0 copy-start.1
  6.5 0.0 reduce-scatter.5.cloned.1.call-start
  6.5 1.4 reshape.19
  7.9 0.0 copy-done.1
  7.9 0.3 convolution_convert_fusion.1
  8.2 0.0 copy-start.3
  8.3 2.4 %collective-permute-start.1 = (bf16[1,16,2,256]{3,1,2,0:T(8,128)(2,1)S(1)}, bf16[1,16,2,256]{3,1,2,0:T(8,128)(2,1)S(1)}, u32[]{:S(2)}, u32[]{:S(2)}) collective-permute-start(bf16[1,16,2,256]{3,1,2,0:T(8,128)(2,1)S(1)} %copy.41), channel_id=1, source_target_pairs={{0,4},{4,8},{8,12},{1,5},{5,9},{9,13},{2,6},{6,10},{10,14},{3,7},{... | collective-permute-start | bytes 49160 | tf_op jit(solution)/shard_map/ppermute | solution.py:21
  10.7 1.3 collective-permute-start
  12.0 0.1 reshape.20
  12.2 0.0 collective-permute-done.1
  12.2 0.0 copy-start.2
  12.2 0.0 copy-start.4
  12.2 0.1 constant_dynamic-update-slice_fusion.1
  12.3 3.7 %collective-permute-done = bf16[1,16,2,256]{3,1,2,0:T(8,128)(2,1)S(1)} collective-permute-done((bf16[1,16,2,256]{3,1,2,0:T(8,128)(2,1)S(1)}, bf16[1,16,2,256]{3,1,2,0:T(8,128)(2,1)S(1)}, u32[]{:S(2)}, u32[]{:S(2)}) %collective-permute-start) | collective-permute-done | bytes 16416 | tf_op jit(solution)/shard_map/ppermute | solution.py:22
  15.9 0.1 fusion.51
  16.0 1.3 collective-permute-start.2
  17.3 4.5 %collective-permute-start.3 = (bf16[18,1,2,256]{3,1,2,0:T(2,128)(2,1)S(1)}, bf16[18,1,2,256]{3,1,2,0:T(2,128)(2,1)S(1)}, u32[]{:S(2)}, u32[]{:S(2)}) collective-permute-start(bf16[18,1,2,256]{3,1,2,0:T(2,128)(2,1)S(1)} %get-tuple-element.7), channel_id=1, source_target_pairs={{0,1},{1,2},{2,3},{4,5},{5,6},{6,7},{8,9},{9,10},{10,11},{12,13},{... | collective-permute-start | bytes 55304 | tf_op jit(solution)/shard_map/ppermute | solution.py:21
  21.8 0.0 copy-done.3
  21.9 0.0 collective-permute-done.2
  21.9 1.6 collective-permute-done.3
  23.5 0.3 select_maximum_fusion.2
  23.8 0.0 copy-done.2
  23.8 0.0 copy-done.4
  23.8 1.9 %convolution_bitcast_fusion.1 = f32[256,512]{1,0:T(8,128)} fusion(bf16[16,16,2,512]{3,2,1,0:T(2,128)(2,1)S(1)} %copy-done.2, bf16[16,16,2,256]{3,1,2,0:T(8,128)(2,1)S(1)} %get-tuple-element.16, bf16[18,18,4,256]{3,1,2,0:T(8,128)(2,1)S(1)} %select_maximum_fusion.2, bf16[18,16,2,256]{3,1,2,0:T(8,128)(2,1)S(1)} %constant_dynamic-update-slice_fusion, ...), kind=kOutput, calls=%fused_computation.4 | convolution fusion | flops 139984896 | bytes 2255872 | tf_op jit(solution)/shard_map/dot_general | solution.py:74
  25.7 0.0 reduce-scatter.5.cloned.1.call-update
  25.7 0.0 reduce-scatter.7.cloned.1.call-start
  25.7 24.7 %reduce-scatter.5.cloned.1.call-done = f32[64,512]{1,0:T(8,128)} async-done(((f32[256,512]{1,0:T(8,128)}), f32[64,512]{1,0:T(8,128)}) %reduce-scatter.5.cloned.1.call-update) | async-done | bytes 131088 | tf_op jit(solution)/shard_map/reduce_scatter | solution.py:73
  50.4 0.0 reduce-scatter.7.cloned.1.call-update
  50.4 0.0 reduce-scatter.9.cloned.1.call-start
  50.5 21.6 %reduce-scatter.7.cloned.1.call-done = f32[16,512]{1,0:T(8,128)} async-done(((f32[64,512]{1,0:T(8,128)}), f32[16,512]{1,0:T(8,128)}) %reduce-scatter.7.cloned.1.call-update) | async-done | bytes 32784 | tf_op jit(solution)/shard_map/reduce_scatter | solution.py:81
  72.1 0.0 copy-done
  72.1 1.7 fusion.55
  73.9 30.9 %all_gather.3 = bf16[256,512]{1,0:T(8,128)(2,1)S(1)} all-gather(bf16[16,512]{1,0:T(8,128)(2,1)S(1)} %get-tuple-element.20), channel_id=1, replica_groups=mesh['groups'=2,'wide'=4,'narrow'=4] {'wide','narrow'}, dimensions={0}, use_global_device_ids=true | all-gather | bytes 278528 | tf_op jit(solution)/shard_map/all_gather | solution.py:85
  104.7 0.3 fusion.1
  105.1 0.1 fusion.52
  105.2 0.1 copy.50
  105.3 1.3 collective-permute-start.5
  106.6 0.1 copy.46
  106.7 0.1 reshape.21
  106.8 0.1 copy.47
  107.0 1.3 collective-permute-start.4
  108.3 0.0 collective-permute-done.5
  108.3 0.1 constant_dynamic-update-slice_fusion.4
  108.4 3.7 %collective-permute-done.4 = bf16[1,16,2,256]{3,1,2,0:T(8,128)(2,1)S(1)} collective-permute-done((bf16[1,16,2,256]{3,1,2,0:T(8,128)(2,1)S(1)}, bf16[1,16,2,256]{3,1,2,0:T(8,128)(2,1)S(1)}, u32[]{:S(2)}, u32[]{:S(2)}) %collective-permute-start.4) | collective-permute-done | bytes 16416 | tf_op jit(solution)/shard_map/ppermute | solution.py:22
  112.0 0.1 fusion.50
  112.1 1.3 collective-permute-start.6
  113.4 4.5 %collective-permute-start.7 = (bf16[18,1,2,256]{3,1,2,0:T(2,128)(2,1)S(1)}, bf16[18,1,2,256]{3,1,2,0:T(2,128)(2,1)S(1)}, u32[]{:S(2)}, u32[]{:S(2)}) collective-permute-start(bf16[18,1,2,256]{3,1,2,0:T(2,128)(2,1)S(1)} %get-tuple-element.5), channel_id=1, source_target_pairs={{0,1},{1,2},{2,3},{4,5},{5,6},{6,7},{8,9},{9,10},{10,11},{12,13},{... | collective-permute-start | bytes 55304 | tf_op jit(solution)/shard_map/ppermute | solution.py:21
  118.0 0.0 collective-permute-done.6
  118.0 1.6 collective-permute-done.7
  119.6 0.3 select_maximum_fusion
  119.9 1.9 %convolution_bitcast_fusion = f32[256,512]{1,0:T(8,128)} fusion(bf16[16,16,2,512]{3,2,1,0:T(2,128)(2,1)S(1)} %copy-done.2, bf16[16,16,2,256]{3,1,2,0:T(8,128)(2,1)S(1)} %get-tuple-element.12, bf16[18,18,4,256]{3,1,2,0:T(8,128)(2,1)S(1)} %select_maximum_fusion, bf16[18,16,2,256]{3,1,2,0:T(8,128)(2,1)S(1)} %constant_dynamic-update-slice_fusion.3, ...), kind=kOutput, calls=%fused_computation.3 | convolution fusion | flops 139984896 | bytes 2255872 | tf_op jit(solution)/shard_map/dot_general | solution.py:74
  121.8 0.0 reduce-scatter.9.cloned.1.call-update
  121.8 0.0 reduce-scatter.11.cloned.1.call-start
  121.8 23.6 %reduce-scatter.9.cloned.1.call-done = f32[64,512]{1,0:T(8,128)} async-done(((f32[256,512]{1,0:T(8,128)}), f32[64,512]{1,0:T(8,128)}) %reduce-scatter.9.cloned.1.call-update) | async-done | bytes 131088 | tf_op jit(solution)/shard_map/reduce_scatter | solution.py:73
  145.4 0.0 reduce-scatter.11.cloned.1.call-update
  145.4 21.6 %reduce-scatter.11.cloned.1.call-done = f32[16,512]{1,0:T(8,128)} async-done(((f32[64,512]{1,0:T(8,128)}), f32[16,512]{1,0:T(8,128)}) %reduce-scatter.11.cloned.1.call-update) | async-done | bytes 32784 | tf_op jit(solution)/shard_map/reduce_scatter | solution.py:81
  167.0 2.3 %convolution_add_fusion = f32[16,512]{1,0:T(8,128)} fusion(f32[512,512]{1,0:T(8,128)S(1)} %copy-done, f32[16,512]{1,0:T(8,128)S(1)} %get-tuple-element.21, f32[16,512]{1,0:T(8,128)} %reduce-scatter.11.cloned.1.call-done), kind=kOutput, calls=%fused_computation.8 | convolution fusion | flops 50356224 | bytes 1146880 | tf_op jit(solution)/shard_map/dot_general | solution.py:45
  (14 shorter events, 0.1 us)
Async XLA Ops:
  6.5 65.6 %copy-start = (f32[512,512]{1,0:T(8,128)S(1)}, f32[512,512]{1,0:T(8,128)}, u32[]{:S(2)}) copy-start(f32[512,512]{1,0:T(8,128)} %param.9) | copy-start | bytes 3145732
  6.5 1.4 copy-start.1
  6.5 43.9 %reduce-scatter.5.cloned.1.call-start = ((), (), s32[]{:S(2)}) async-start(), calls=%async_computation.4 | async-start | bytes 655360 | tf_op jit(solution)/shard_map/reduce_scatter | solution.py:73
  8.2 13.6 %copy-start.3 = (f32[3,256]{1,0:T(4,128)S(1)}, f32[3,256]{1,0:T(4,128)}, u32[]{:S(2)}) copy-start(f32[3,256]{1,0:T(4,128)} %param.7) | copy-start | bytes 9220
  8.3 3.9 %collective-permute-start.1 = (bf16[1,16,2,256]{3,1,2,0:T(8,128)(2,1)S(1)}, bf16[1,16,2,256]{3,1,2,0:T(8,128)(2,1)S(1)}, u32[]{:S(2)}, u32[]{:S(2)}) collective-permute-start(bf16[1,16,2,256]{3,1,2,0:T(8,128)(2,1)S(1)} %copy.41), channel_id=1, source_target_pairs={{0,4},{4,8},{8,12},{1,5},{5,9},{9,13},{2,6},{6,10},{10,14},{3,7},{... | collective-permute-start | bytes 49160 | tf_op jit(solution)/shard_map/ppermute | solution.py:21
  10.7 5.2 %collective-permute-start = (bf16[1,16,2,256]{3,1,2,0:T(8,128)(2,1)S(1)}, bf16[1,16,2,256]{3,1,2,0:T(8,128)(2,1)S(1)}, u32[]{:S(2)}, u32[]{:S(2)}) collective-permute-start(bf16[1,16,2,256]{3,1,2,0:T(8,128)(2,1)S(1)} %copy.39), channel_id=1, source_target_pairs={{4,0},{8,4},{12,8},{5,1},{9,5},{13,9},{6,2},{10,6},{14,10},{7,3},{... | collective-permute-start | bytes 49160 | tf_op jit(solution)/shard_map/ppermute | solution.py:22
  12.2 11.6 %copy-start.2 = (bf16[16,16,2,512]{3,2,1,0:T(2,128)(2,1)S(1)}, bf16[16,16,2,512]{3,2,1,0:T(2,128)(2,1)}, u32[]{:S(2)}) copy-start(bf16[16,16,2,512]{3,2,1,0:T(2,128)(2,1)} %param.5) | copy-start | bytes 1572868
  12.2 11.6 %copy-start.4 = (f32[16,16,2]{1,2,0:T(2,128)S(1)}, f32[16,16,2]{1,2,0:T(2,128)}, u32[]{:S(2)}) copy-start(f32[16,16,2]{1,2,0:T(2,128)} %param.6) | copy-start | bytes 6148
  16.0 5.9 %collective-permute-start.2 = (bf16[18,1,2,256]{3,1,2,0:T(2,128)(2,1)S(1)}, bf16[18,1,2,256]{3,1,2,0:T(2,128)(2,1)S(1)}, u32[]{:S(2)}, u32[]{:S(2)}) collective-permute-start(bf16[18,1,2,256]{3,1,2,0:T(2,128)(2,1)S(1)} %get-tuple-element.8), channel_id=1, source_target_pairs={{1,0},{2,1},{3,2},{5,4},{6,5},{7,6},{9,8},{10,9},{11,10},{13,12},{... | collective-permute-start | bytes 55304 | tf_op jit(solution)/shard_map/ppermute | solution.py:22
  17.3 6.2 %collective-permute-start.3 = (bf16[18,1,2,256]{3,1,2,0:T(2,128)(2,1)S(1)}, bf16[18,1,2,256]{3,1,2,0:T(2,128)(2,1)S(1)}, u32[]{:S(2)}, u32[]{:S(2)}) collective-permute-start(bf16[18,1,2,256]{3,1,2,0:T(2,128)(2,1)S(1)} %get-tuple-element.7), channel_id=1, source_target_pairs={{0,1},{1,2},{2,3},{4,5},{5,6},{6,7},{8,9},{9,10},{10,11},{12,13},{... | collective-permute-start | bytes 55304 | tf_op jit(solution)/shard_map/ppermute | solution.py:21
  25.7 46.4 %reduce-scatter.7.cloned.1.call-start = ((), (), s32[]{:S(2)}) async-start(), calls=%async_computation.5 | async-start | bytes 163840 | tf_op jit(solution)/shard_map/reduce_scatter | solution.py:81
  50.4 94.9 %reduce-scatter.9.cloned.1.call-start = ((), (), s32[]{:S(2)}) async-start(), calls=%async_computation.6 | async-start | bytes 655360 | tf_op jit(solution)/shard_map/reduce_scatter | solution.py:73
  105.3 3.0 %collective-permute-start.5 = (bf16[1,16,2,256]{3,1,2,0:T(8,128)(2,1)S(1)}, bf16[1,16,2,256]{3,1,2,0:T(8,128)(2,1)S(1)}, u32[]{:S(2)}, u32[]{:S(2)}) collective-permute-start(bf16[1,16,2,256]{3,1,2,0:T(8,128)(2,1)S(1)} %copy.51), channel_id=1, source_target_pairs={{0,4},{4,8},{8,12},{1,5},{5,9},{9,13},{2,6},{6,10},{10,14},{3,7},{... | collective-permute-start | bytes 49160 | tf_op jit(solution)/shard_map/ppermute | solution.py:21
  107.0 5.1 %collective-permute-start.4 = (bf16[1,16,2,256]{3,1,2,0:T(8,128)(2,1)S(1)}, bf16[1,16,2,256]{3,1,2,0:T(8,128)(2,1)S(1)}, u32[]{:S(2)}, u32[]{:S(2)}) collective-permute-start(bf16[1,16,2,256]{3,1,2,0:T(8,128)(2,1)S(1)} %copy.48), channel_id=1, source_target_pairs={{4,0},{8,4},{12,8},{5,1},{9,5},{13,9},{6,2},{10,6},{14,10},{7,3},{... | collective-permute-start | bytes 49160 | tf_op jit(solution)/shard_map/ppermute | solution.py:22
  112.1 5.9 %collective-permute-start.6 = (bf16[18,1,2,256]{3,1,2,0:T(2,128)(2,1)S(1)}, bf16[18,1,2,256]{3,1,2,0:T(2,128)(2,1)S(1)}, u32[]{:S(2)}, u32[]{:S(2)}) collective-permute-start(bf16[18,1,2,256]{3,1,2,0:T(2,128)(2,1)S(1)} %get-tuple-element.6), channel_id=1, source_target_pairs={{1,0},{2,1},{3,2},{5,4},{6,5},{7,6},{9,8},{10,9},{11,10},{13,12},{... | collective-permute-start | bytes 55304 | tf_op jit(solution)/shard_map/ppermute | solution.py:22
  113.4 6.2 %collective-permute-start.7 = (bf16[18,1,2,256]{3,1,2,0:T(2,128)(2,1)S(1)}, bf16[18,1,2,256]{3,1,2,0:T(2,128)(2,1)S(1)}, u32[]{:S(2)}, u32[]{:S(2)}) collective-permute-start(bf16[18,1,2,256]{3,1,2,0:T(2,128)(2,1)S(1)} %get-tuple-element.5), channel_id=1, source_target_pairs={{0,1},{1,2},{2,3},{4,5},{5,6},{6,7},{8,9},{9,10},{10,11},{12,13},{... | collective-permute-start | bytes 55304 | tf_op jit(solution)/shard_map/ppermute | solution.py:21
  121.8 45.2 %reduce-scatter.11.cloned.1.call-start = ((), (), s32[]{:S(2)}) async-start(), calls=%async_computation.7 | async-start | bytes 163840 | tf_op jit(solution)/shard_map/reduce_scatter | solution.py:81
Sparse Core Ops, SparseCore 0:
  25.8 24.5 reduce-scatter.4
  52.7 19.4 reduce-scatter.6
  121.9 23.4 reduce-scatter.8
  147.5 19.4 reduce-scatter.10
where the time goes:
time: 176 us
  waiting for transfers between devices  102 us (58%)
  blocking collectives  30.9 us (18%)
  starting transfers between devices  18.1 us (10%)
  between operations  13.4 us (8%)
  matrix products  8.48 us (5%)
  local copies, waits for them, and re-layouts  2.33 us (1%)
    reduce_scatter x2, waiting for transfers between devices, body(): lax.psum_scatter(lax.dot_general(forcing, flat_basis, (((0,), (0,)), ((),...  48.2 us
    reduce_scatter x2, waiting for transfers between devices, body(): lax.psum_scatter(partial_rows, 'narrow', scatter_dimension=0, tiled=True)  43.2 us
    all_gather x1, blocking collectives, body(): lax.all_gather(state.astype(jnp.bfloat16), ('wide', 'narrow'), axis=0, ti...  30.9 us
    ppermute x4, starting transfers between devices, padded_2(): before = lax.ppermute(last, axis, up)  12.8 us
    ppermute x4, waiting for transfers between devices, padded_2(): after = lax.ppermute(first, axis, down)  7.34 us
    ppermute x4, starting transfers between devices, padded_2(): after = lax.ppermute(first, axis, down)  5.17 us
    dot_general x2, matrix products, advance(): jnp.dot(update, propagator.T, precision=lax.Precision.HIGHEST, preferred_...  4.07 us
    dot_general x2, matrix products, body(): lax.dot_general(forcing, flat_basis, (((0,), (0,)), ((), ())), preferred_...  3.75 us
  transfers between devices with their start and end apart: 12, of which 8 were waited for; matrix products, arithmetic and copies ran while one was open for 0% of the time, Pallas kernels for 0%

commit v1 on v0

v1 whole, which is shorter than its diff:
```python
import functools
import math

import jax
import jax.numpy as jnp
from jax import lax
from jax.experimental import pallas as pl
from jax.experimental.pallas import tpu as pltpu
from jax.sharding import PartitionSpec as P

ITERS = 2
WIRE = jnp.float32
PAD = 8

step_size = 4.0

NT = (((1,), (1,)), ((), ()))
NN = (((1,), (0,)), ((), ()))


def peer(me, offset):
    result, bit = me, 1
    while bit <= offset:
        if offset & bit:
            result = result + (1 - 2 * ((me // bit) % 2)) * bit
        bit *= 2
    return result


def dot(a, b, dims):
    return lax.dot_general(a, b, dims, preferred_element_type=jnp.float32)


def kernel(
    sizes, wide, narrow, scale,
    basis_ref, kappa_ref, velocity_ref, coefficients_ref, propagator_ref, out_ref,
    faces, halo_x, halo_y, field, forcing_ref, turned, g_high, g_low,
    partial, landed_w, reduced, landed_n, gathered,
    halo_send, halo_recv, w_send, w_recv, n_send, n_recv, an_send, an_recv, aw_send, aw_recv,
):
    size_x, size_y, size_z = sizes
    rows = size_y * size_z
    samples, modes = coefficients_ref.shape
    owned = samples // (wide * narrow)
    chunk = owned * narrow
    me_w, me_n = lax.axis_index("wide"), lax.axis_index("narrow")

    halo_x[...] = jnp.zeros_like(halo_x)
    halo_y[...] = jnp.zeros_like(halo_y)
    barrier = pltpu.get_barrier_semaphore()
    for e in range(1, wide):
        pl.semaphore_signal(barrier, inc=1, device_id={"wide": peer(me_w, e)}, device_id_type=pl.DeviceIdType.MESH)
    for d in range(1, narrow):
        pl.semaphore_signal(barrier, inc=1, device_id={"narrow": peer(me_n, d)}, device_id_type=pl.DeviceIdType.MESH)

    for x in range(size_x):
        at = x * rows
        faces[0, x * size_z:(x + 1) * size_z, :] = basis_ref[at:at + size_z, :]
        faces[1, x * size_z:(x + 1) * size_z, :] = basis_ref[at + rows - size_z:at + rows, :]
    g_high[...] = propagator_ref[...].astype(jnp.bfloat16)
    g_low[...] = (propagator_ref[...] - g_high[...].astype(jnp.float32)).astype(jnp.bfloat16)

    pl.semaphore_wait(barrier, wide + narrow - 2)

    def remote(src, dst, send, recv, **where):
        return pltpu.make_async_remote_copy(
            src_ref=src, dst_ref=dst, send_sem=send, recv_sem=recv,
            device_id=where, device_id_type=pl.DeviceIdType.MESH,
        )

    last = (size_x - 1) * rows
    halos = (
        (remote(faces.at[1], halo_y.at[0], halo_send.at[0], halo_recv.at[0], narrow=lax.rem(me_n + 1, narrow)),
         me_n < narrow - 1, me_n > 0),
        (remote(faces.at[0], halo_y.at[1], halo_send.at[1], halo_recv.at[1], narrow=lax.rem(me_n + narrow - 1, narrow)),
         me_n > 0, me_n < narrow - 1),
        (remote(basis_ref.at[pl.ds(last, rows)], halo_x.at[0], halo_send.at[2], halo_recv.at[2], wide=lax.rem(me_w + 1, wide)),
         me_w < wide - 1, me_w > 0),
        (remote(basis_ref.at[pl.ds(0, rows)], halo_x.at[1], halo_send.at[3], halo_recv.at[3], wide=lax.rem(me_w + wide - 1, wide)),
         me_w > 0, me_w < wide - 1),
    )
    for copy, sends, receives in halos:
        pl.when(sends)(copy.start)

    z_index = lax.broadcasted_iota(jnp.int32, (rows, samples), 0) % size_z
    first_row = (me_w * narrow + me_n) * owned
    if owned % 8 == 0:
        first_row = pl.multiple_of(first_row, 8)
    state = coefficients_ref[pl.ds(first_row, owned), :]
    lift_rows = coefficients_ref[...].astype(jnp.bfloat16)
    pending = []

    def lifted(of):
        return dot(of, lift_rows, NT).astype(jnp.bfloat16).astype(jnp.float32)

    for step in range(ITERS):
        field[1:size_x + 1, PAD:PAD + rows, :] = lifted(basis_ref[...]).reshape(size_x, rows, samples)
        if step == 0:
            for copy, sends, receives in halos:
                pl.when(receives)(copy.wait_recv)
        field[0, PAD:PAD + rows, :] = lifted(halo_x[0])
        field[size_x + 1, PAD:PAD + rows, :] = lifted(halo_x[1])
        before, after = lifted(halo_y[0]), lifted(halo_y[1])
        for x in range(size_x):
            field[x + 1, PAD - size_z:PAD, :] = before[x * size_z:(x + 1) * size_z]
            field[x + 1, PAD + rows:PAD + rows + size_z, :] = after[x * size_z:(x + 1) * size_z]

        def slab(x, carry):
            center = field[x + 1, PAD:PAD + rows, :]
            x_next = field[x + 2, PAD:PAD + rows, :]
            x_prev = field[x, PAD:PAD + rows, :]
            y_next = field[x + 1, PAD + size_z:PAD + rows + size_z, :]
            y_prev = field[x + 1, PAD - size_z:PAD + rows - size_z, :]
            z_next = jnp.where(z_index < size_z - 1, field[x + 1, PAD + 1:PAD + rows + 1, :], 0.0)
            z_prev = jnp.where(z_index > 0, field[x + 1, PAD - 1:PAD + rows - 1, :], 0.0)
            spread = x_next + x_prev + y_next + y_prev + z_next + z_prev - 6.0 * center
            carried = velocity_ref[0:1, :] * (x_next * x_next - x_prev * x_prev)
            carried = carried + velocity_ref[1:2, :] * (y_next * y_next - y_prev * y_prev)
            carried = carried + velocity_ref[2:3, :] * (z_next * z_next - z_prev * z_prev)
            at = pl.multiple_of(x * rows, rows)
            result = kappa_ref[pl.ds(at, rows), :] * spread - 0.25 * carried
            forcing_ref[pl.ds(at, rows), :] = result.astype(jnp.bfloat16)
            return carry

        lax.fori_loop(0, size_x, slab, 0, unroll=4)
        turned[...] = forcing_ref[...].T

        def projected(target):
            at = pl.multiple_of(target * chunk, chunk)
            return dot(turned[pl.ds(at, chunk), :], basis_ref[...], NN)

        copies = []
        for e in reversed(range(1, wide)):
            target = peer(me_w, e)
            partial[step, e - 1] = projected(target).astype(WIRE)
            copy = remote(partial.at[step, e - 1], landed_w.at[step, e - 1], w_send.at[step, e - 1], w_recv.at[step, e - 1], wide=target)
            copy.start()
            copies.append((e, copy))
        total = projected(me_w)
        for e, copy in reversed(copies):
            copy.wait_recv()
            total = total + landed_w[step, e - 1].astype(jnp.float32)
            pending.append(copy)
        for n in range(narrow):
            reduced[step, n] = total[n * owned:(n + 1) * owned].astype(WIRE)
        copies = []
        for d in reversed(range(1, narrow)):
            target = peer(me_n, d)
            copy = remote(reduced.at[step, target], landed_n.at[step, d - 1], n_send.at[step, d - 1], n_recv.at[step, d - 1], narrow=target)
            copy.start()
            copies.append((d, copy))
        summed = reduced[step, me_n].astype(jnp.float32)
        for d, copy in reversed(copies):
            copy.wait_recv()
            summed = summed + landed_n[step, d - 1].astype(jnp.float32)
            pending.append(copy)

        update = state + step_size * (summed * scale)
        high = update.astype(jnp.bfloat16)
        low = (update - high.astype(jnp.float32)).astype(jnp.bfloat16)
        small = dot(high, g_low[...], NT) + dot(low, g_high[...], NT)
        state = update + (dot(high, g_high[...], NT) + small)

        if step + 1 < ITERS:
            gathered[step, me_w, me_n] = state.astype(jnp.bfloat16)
            along = []
            for d in reversed(range(1, narrow)):
                block = gathered.at[step, me_w, me_n]
                copy = remote(block, block, an_send.at[step, d - 1], an_recv.at[step, d - 1], narrow=peer(me_n, d))
                copy.start()
                along.append((d, copy))
            across = []

            def forward(d):
                block = gathered.at[step, me_w, peer(me_n, d)]
                for e in reversed(range(1, wide)):
                    copy = remote(block, block, aw_send.at[step, e - 1, d], aw_recv.at[step, e - 1, d], wide=peer(me_w, e))
                    copy.start()
                    across.append(copy)

            forward(0)
            for d, copy in reversed(along):
                copy.wait_recv()
                pending.append(copy)
                forward(d)
            for copy in across:
                copy.wait_recv()
                pending.append(copy)
            lift_rows = gathered[step].reshape(samples, modes)

    out_ref[...] = state
    for copy in pending:
        copy.wait_send()
    for copy, sends, receives in halos:
        pl.when(sends)(copy.wait_send)


def body(basis, kappa, velocity, coefficients, propagator):
    size_x, size_y, size_z, modes = basis.shape
    samples = coefficients.shape[0]
    wide, narrow = lax.axis_size("wide"), lax.axis_size("narrow")
    owned = samples // (wide * narrow)
    chunk = owned * narrow
    cells, rows = size_x * size_y * size_z, size_y * size_z
    scale = 1.0 / math.sqrt(cells * wide * narrow)
    f32, bf16 = jnp.float32, jnp.bfloat16
    dma = pltpu.SemaphoreType.DMA
    vmem = pl.BlockSpec(memory_space=pltpu.VMEM)
    return pl.pallas_call(
        functools.partial(kernel, (size_x, size_y, size_z), wide, narrow, scale),
        out_shape=jax.ShapeDtypeStruct((owned, modes), f32),
        in_specs=[vmem] * 5,
        out_specs=vmem,
        scratch_shapes=[
            pltpu.VMEM((2, size_x * size_z, modes), bf16),
            pltpu.VMEM((2, rows, modes), bf16),
            pltpu.VMEM((2, size_x * size_z, modes), bf16),
            pltpu.VMEM((size_x + 2, rows + 2 * PAD, samples), f32),
            pltpu.VMEM((cells, samples), bf16),
            pltpu.VMEM((samples, cells), bf16),
            pltpu.VMEM((modes, modes), bf16),
            pltpu.VMEM((modes, modes), bf16),
            pltpu.VMEM((ITERS, wide - 1, chunk, modes), WIRE),
            pltpu.VMEM((ITERS, wide - 1, chunk, modes), WIRE),
            pltpu.VMEM((ITERS, narrow, owned, modes), WIRE),
            pltpu.VMEM((ITERS, narrow - 1, owned, modes), WIRE),
            pltpu.VMEM((ITERS - 1, wide, narrow, owned, modes), bf16),
            dma((4,)), dma((4,)),
            dma((ITERS, wide - 1)), dma((ITERS, wide - 1)),
            dma((ITERS, narrow - 1)), dma((ITERS, narrow - 1)),
            dma((ITERS - 1, narrow - 1)), dma((ITERS - 1, narrow - 1)),
            dma((ITERS - 1, wide - 1, narrow)), dma((ITERS - 1, wide - 1, narrow)),
        ],
        compiler_params=pltpu.CompilerParams(
            collective_id=0, has_side_effects=True, vmem_limit_bytes=48 * 1024 * 1024
        ),
    )(basis.reshape(cells, modes), kappa.reshape(cells, 1), velocity, coefficients, propagator)


def solution(mesh):
    placed = (
        P(("groups", "wide"), "narrow", None, None),
        P(("groups", "wide"), "narrow", None),
        P(None, "groups"),
        P("groups", None),
        P("groups", None),
    )
    return jax.shard_map(
        body,
        mesh=mesh,
        in_specs=placed,
        out_specs=P(("groups", "wide", "narrow"), None),
        check_vma=False,
    )
```

time: 176 us -> 45.9 us (0.26)
  waiting for transfers between devices: 102 us -> 0 us
  Pallas kernels: 0 us -> 42.6 us
  blocking collectives: 30.9 us -> 0 us
  starting transfers between devices: 18.1 us -> 0 us
  between operations: 13.4 us -> 0.06 us
  matrix products: 8.48 us -> 0 us
    reduce_scatter x4 -> x0, waiting for transfers between devices: 91.4 us -> none  [the longest x2 48.2 us: body(): lax.psum_scatter(lax.dot_general(forcing, flat_basis, (((0,), (0,)), ((),...]
    pallas_call x0 -> x1, Pallas kernels: none -> 42.6 us  [body(): pl.pallas_call(functools.partial(kernel, (size_x, size_y, size_z), wide,...]
    all_gather x1 -> x0, blocking collectives: 30.9 us -> none  [body(): lax.all_gather(state.astype(jnp.bfloat16), ('wide', 'narrow'), axis=0, ti...]
    ppermute x8 -> x0, starting transfers between devices: 18 us -> none  [the longest x4 12.8 us: padded_2(): before = lax.ppermute(last, axis, up)]
    ppermute x8 -> x0, waiting for transfers between devices: 10.5 us -> none  [the longest x4 7.34 us: padded_2(): after = lax.ppermute(first, axis, down)]
    dot_general x6 -> x0, matrix products: 8.48 us -> none  [the longest x2 4.07 us: advance(): jnp.dot(update, propagator.T, precision=lax.Precision.HIGHEST, preferred_...]
  transfers between devices with their start and end apart: 12 -> 0, of which waited for: 8 -> 0; matrix products, arithmetic and copies ran while one was open for 0% -> 0% of each run, Pallas kernels for 0% -> 0%
where the time goes in v1:
time: 45.9 us; the launch traced here: 45.7 us
  Pallas kernels  42.6 us (93%)
  local copies, waits for them, and re-layouts  3 us (7%)
    pallas_call x1, Pallas kernels, body(): pl.pallas_call(functools.partial(kernel, (size_x, size_y, size_z), wide,...  42.6 us
    unnamed x8, local copies, waits for them, and re-layouts  1.6 us
    reshape x1, local copies, waits for them, and re-layouts, body(): basis.reshape(cells, modes)  1.3 us

profile of v1, /device:TPU:0, one launch (start us, length us, event | category | flops | bytes accessed | tf_op | source)
XLA Modules:
  0.0 45.7 jit_solution(10500123101867874678)
XLA Ops:
  0.0 0.0 copy-start
  0.0 1.0 %copy.7 = f32[16,16,2]{2,1,0:T(8,128)S(1)} copy(f32[16,16,2]{1,2,0:T(2,128)} %param.6) | data formatting | bytes 4096 | tf_op args[1]
  1.0 0.1 reshape.8.kappa_ref
  1.1 0.0 copy-start.1
  1.1 0.0 copy-start.2
  1.1 1.3 %reshape.6.basis_ref = bf16[512,512]{1,0:T(8,128)(2,1)S(1)} reshape(bf16[16,16,2,512]{3,2,1,0:T(2,128)(2,1)} %param.5) | data formatting | bytes 1048576 | tf_op jit(solution)/shard_map/reshape | solution.py:237
  2.4 0.0 copy-done
  2.4 0.0 copy-done.1
  2.4 0.0 copy-done.2
  2.4 42.6 %shard_map.55 = f32[16,512]{1,0:T(8,128)S(1)} custom-call(bf16[512,512]{1,0:T(8,128)(2,1)S(1)} %reshape.6.basis_ref, f32[512,1]{1,0:T(8,128)S(1)} %reshape.8.kappa_ref, f32[3,256]{1,0:T(4,128)S(1)} %copy-done.2, f32[256,512]{1,0:T(8,128)S(1)} %copy-done.1, f32[512,512]{1,0:T(8,128)S(1)} %copy-done), custom_call_target="tpu_custom_call" | custom-call | tf_op jit(solution)/shard_map/pallas_call | solution.py:209
  45.1 0.6 %copy.10 = f32[16,512]{1,0:T(8,128)} copy(f32[16,512]{1,0:T(8,128)S(1)} %shard_map.55) | data formatting | bytes 65536
Async XLA Ops:
  0.0 2.4 %copy-start = (f32[512,512]{1,0:T(8,128)S(1)}, f32[512,512]{1,0:T(8,128)}, u32[]{:S(2)}) copy-start(f32[512,512]{1,0:T(8,128)} %propagator_ref.1) | copy-start | bytes 3145732
  1.1 1.3 %copy-start.1 = (f32[256,512]{1,0:T(8,128)S(1)}, f32[256,512]{1,0:T(8,128)}, u32[]{:S(2)}) copy-start(f32[256,512]{1,0:T(8,128)} %coefficients_ref.1) | copy-start | bytes 1572868
  1.1 1.3 %copy-start.2 = (f32[3,256]{1,0:T(4,128)S(1)}, f32[3,256]{1,0:T(4,128)}, u32[]{:S(2)}) copy-start(f32[3,256]{1,0:T(4,128)} %velocity_ref.1) | copy-start | bytes 9220

commit v2 on v1

--- a/solution.py
+++ b/solution.py
@@ -9,7 +9,7 @@
 from jax.sharding import PartitionSpec as P
 
 ITERS = 2
-WIRE = jnp.float32
+WIRE = jnp.bfloat16
 PAD = 8
 
 step_size = 4.0
@@ -35,8 +35,8 @@
     sizes, wide, narrow, scale,
     basis_ref, kappa_ref, velocity_ref, coefficients_ref, propagator_ref, out_ref,
     faces, halo_x, halo_y, field, forcing_ref, turned, g_high, g_low,
-    partial, landed_w, reduced, landed_n, gathered,
-    halo_send, halo_recv, w_send, w_recv, n_send, n_recv, an_send, an_recv, aw_send, aw_recv,
+    pair_out, pair_in, reduced, kept, landed, gathered,
+    halo_send, halo_recv, pair_send, pair_recv, r_send, r_recv, g_send, g_recv, f_send, f_recv,
 ):
     size_x, size_y, size_z = sizes
     rows = size_y * size_z
@@ -48,10 +48,12 @@
     halo_x[...] = jnp.zeros_like(halo_x)
     halo_y[...] = jnp.zeros_like(halo_y)
     barrier = pltpu.get_barrier_semaphore()
-    for e in range(1, wide):
-        pl.semaphore_signal(barrier, inc=1, device_id={"wide": peer(me_w, e)}, device_id_type=pl.DeviceIdType.MESH)
-    for d in range(1, narrow):
-        pl.semaphore_signal(barrier, inc=1, device_id={"narrow": peer(me_n, d)}, device_id_type=pl.DeviceIdType.MESH)
+    greeted = [(e, 0) for e in range(1, wide)] + [(e, d) for e in range(0, wide, 2) for d in range(1, narrow)]
+    for e, d in greeted:
+        pl.semaphore_signal(
+            barrier, inc=1, device_id={"wide": peer(me_w, e), "narrow": peer(me_n, d)},
+            device_id_type=pl.DeviceIdType.MESH,
+        )
 
     for x in range(size_x):
         at = x * rows
@@ -60,7 +62,7 @@
     g_high[...] = propagator_ref[...].astype(jnp.bfloat16)
     g_low[...] = (propagator_ref[...] - g_high[...].astype(jnp.float32)).astype(jnp.bfloat16)
 
-    pl.semaphore_wait(barrier, wide + narrow - 2)
+    pl.semaphore_wait(barrier, len(greeted))
 
     def remote(src, dst, send, recv, **where):
         return pltpu.make_async_remote_copy(
@@ -129,31 +131,41 @@
             at = pl.multiple_of(target * chunk, chunk)
             return dot(turned[pl.ds(at, chunk), :], basis_ref[...], NN)
 
-        copies = []
-        for e in reversed(range(1, wide)):
-            target = peer(me_w, e)
-            partial[step, e - 1] = projected(target).astype(WIRE)
-            copy = remote(partial.at[step, e - 1], landed_w.at[step, e - 1], w_send.at[step, e - 1], w_recv.at[step, e - 1], wide=target)
+        pairs = []
+        for i in reversed(range(wide // 2)):
+            pair_out[step, i] = projected(peer(me_w, 2 * i + 1))
+            copy = remote(
+                pair_out.at[step, i], pair_in.at[step, i], pair_send.at[step, i], pair_recv.at[step, i],
+                wide=peer(me_w, 1),
+            )
             copy.start()
-            copies.append((e, copy))
-        total = projected(me_w)
-        for e, copy in reversed(copies):
+            pairs.append((i, copy))
+        totals = [projected(peer(me_w, 2 * i)) for i, copy in pairs]
+        spread_out = []
+        for (i, copy), total in zip(pairs, totals):
             copy.wait_recv()
-            total = total + landed_w[step, e - 1].astype(jnp.float32)
             pending.append(copy)
-        for n in range(narrow):
-            reduced[step, n] = total[n * owned:(n + 1) * owned].astype(WIRE)
-        copies = []
-        for d in reversed(range(1, narrow)):
-            target = peer(me_n, d)
-            copy = remote(reduced.at[step, target], landed_n.at[step, d - 1], n_send.at[step, d - 1], n_recv.at[step, d - 1], narrow=target)
-            copy.start()
-            copies.append((d, copy))
-        summed = reduced[step, me_n].astype(jnp.float32)
-        for d, copy in reversed(copies):
+            total = total + pair_in[step, i]
+            for n in range(narrow):
+                block = total[n * owned:(n + 1) * owned]
+                reduced[step, i, n] = block.astype(WIRE)
+                if i == 0:
+                    kept[n] = block
+            for d in reversed(range(narrow)):
+                if i == 0 and d == 0:
+                    continue
+                copy = remote(
+                    reduced.at[step, i, peer(me_n, d)], landed.at[step, i, d],
+                    r_send.at[step, i, d], r_recv.at[step, i, d],
+                    wide=peer(me_w, 2 * i), narrow=peer(me_n, d),
+                )
+                copy.start()
+                spread_out.append((i, d, copy))
+        summed = kept[me_n]
+        for i, d, copy in reversed(spread_out):
             copy.wait_recv()
-            summed = summed + landed_n[step, d - 1].astype(jnp.float32)
             pending.append(copy)
+            summed = summed + landed[step, i, d].astype(jnp.float32)
 
         update = state + step_size * (summed * scale)
         high = update.astype(jnp.bfloat16)
@@ -163,27 +175,28 @@
 
         if step + 1 < ITERS:
             gathered[step, me_w, me_n] = state.astype(jnp.bfloat16)
-            along = []
-            for d in reversed(range(1, narrow)):
-                block = gathered.at[step, me_w, me_n]
-                copy = remote(block, block, an_send.at[step, d - 1], an_recv.at[step, d - 1], narrow=peer(me_n, d))
+            others = [(i, d) for d in range(narrow) for i in range(wide // 2) if i + d > 0]
+            direct, inside = {}, []
+            own = gathered.at[step, me_w, me_n]
+            for i, d in reversed(others):
+                direct[i, d] = remote(
+                    own, own, g_send.at[step, i, d], g_recv.at[step, i, d],
+                    wide=peer(me_w, 2 * i), narrow=peer(me_n, d),
+                )
+                direct[i, d].start()
+
+            def beside(i, d):
+                block = gathered.at[step, peer(me_w, 2 * i), peer(me_n, d)]
+                copy = remote(block, block, f_send.at[step, i, d], f_recv.at[step, i, d], wide=peer(me_w, 1))
                 copy.start()
-                along.append((d, copy))
-            across = []
-
-            def forward(d):
-                block = gathered.at[step, me_w, peer(me_n, d)]
-                for e in reversed(range(1, wide)):
-                    copy = remote(block, block, aw_send.at[step, e - 1, d], aw_recv.at[step, e - 1, d], wide=peer(me_w, e))
-                    copy.start()
-                    across.append(copy)
-
-            forward(0)
-            for d, copy in reversed(along):
-                copy.wait_recv()
-                pending.append(copy)
-                forward(d)
-            for copy in across:
+                inside.append(copy)
+
+            beside(0, 0)
+            for i, d in others:
+                direct[i, d].wait_recv()
+                pending.append(direct[i, d])
+                beside(i, d)
+            for copy in inside:
                 copy.wait_recv()
                 pending.append(copy)
             lift_rows = gathered[step].reshape(samples, modes)
@@ -220,16 +233,17 @@
             pltpu.VMEM((samples, cells), bf16),
             pltpu.VMEM((modes, modes), bf16),
             pltpu.VMEM((modes, modes), bf16),
-            pltpu.VMEM((ITERS, wide - 1, chunk, modes), WIRE),
-            pltpu.VMEM((ITERS, wide - 1, chunk, modes), WIRE),
-            pltpu.VMEM((ITERS, narrow, owned, modes), WIRE),
-            pltpu.VMEM((ITERS, narrow - 1, owned, modes), WIRE),
+            pltpu.VMEM((ITERS, wide // 2, chunk, modes), f32),
+            pltpu.VMEM((ITERS, wide // 2, chunk, modes), f32),
+            pltpu.VMEM((ITERS, wide // 2, narrow, owned, modes), WIRE),
+            pltpu.VMEM((narrow, owned, modes), f32),
+            pltpu.VMEM((ITERS, wide // 2, narrow, owned, modes), WIRE),
             pltpu.VMEM((ITERS - 1, wide, narrow, owned, modes), bf16),
             dma((4,)), dma((4,)),
-            dma((ITERS, wide - 1)), dma((ITERS, wide - 1)),
-            dma((ITERS, narrow - 1)), dma((ITERS, narrow - 1)),
-            dma((ITERS - 1, narrow - 1)), dma((ITERS - 1, narrow - 1)),
-            dma((ITERS - 1, wide - 1, narrow)), dma((ITERS - 1, wide - 1, narrow)),
+            dma((ITERS, wide // 2)), dma((ITERS, wide // 2)),
+            dma((ITERS, wide // 2, narrow)), dma((ITERS, wide // 2, narrow)),
+            dma((ITERS - 1, wide // 2, narrow)), dma((ITERS - 1, wide // 2, narrow)),
+            dma((ITERS - 1, wide // 2, narrow)), dma((ITERS - 1, wide // 2, narrow)),
         ],
         compiler_params=pltpu.CompilerParams(
             collective_id=0, has_side_effects=True, vmem_limit_bytes=48 * 1024 * 1024

time: 45.9 us -> 34.7 us (0.76)
  Pallas kernels: 42.6 us -> 31.4 us
    pallas_call x1, Pallas kernels: 42.6 us -> 31.4 us  [body(): pl.pallas_call(functools.partial(kernel, (size_x, size_y, size_z), wide,...]
where the time goes in v2:
time: 34.7 us; the launch traced here: 34.5 us
  Pallas kernels  31.4 us (90%)
  local copies, waits for them, and re-layouts  3 us (9%)
    pallas_call x1, Pallas kernels, body(): pl.pallas_call(functools.partial(kernel, (size_x, size_y, size_z), wide,...  31.4 us
    unnamed x8, local copies, waits for them, and re-layouts  1.6 us
    reshape x1, local copies, waits for them, and re-layouts, body(): basis.reshape(cells, modes)  1.3 us

profile of v2, /device:TPU:0, one launch (start us, length us, event | category | flops | bytes accessed | tf_op | source)
XLA Modules:
  0.0 34.5 jit_solution(9242371018261072477)
XLA Ops:
  0.0 0.0 copy-start
  0.0 1.0 %copy.7 = f32[16,16,2]{2,1,0:T(8,128)S(1)} copy(f32[16,16,2]{1,2,0:T(2,128)} %param.6) | data formatting | bytes 4096 | tf_op args[1]
  1.0 0.1 reshape.8.kappa_ref
  1.1 0.0 copy-start.1
  1.1 0.0 copy-start.2
  1.1 1.3 %reshape.6.basis_ref = bf16[512,512]{1,0:T(8,128)(2,1)S(1)} reshape(bf16[16,16,2,512]{3,2,1,0:T(2,128)(2,1)} %param.5) | data formatting | bytes 1048576 | tf_op jit(solution)/shard_map/reshape | solution.py:251
  2.4 0.0 copy-done
  2.4 0.0 copy-done.1
  2.4 0.0 copy-done.2
  2.4 31.4 %shard_map.55 = f32[16,512]{1,0:T(8,128)S(1)} custom-call(bf16[512,512]{1,0:T(8,128)(2,1)S(1)} %reshape.6.basis_ref, f32[512,1]{1,0:T(8,128)S(1)} %reshape.8.kappa_ref, f32[3,256]{1,0:T(4,128)S(1)} %copy-done.2, f32[256,512]{1,0:T(8,128)S(1)} %copy-done.1, f32[512,512]{1,0:T(8,128)S(1)} %copy-done), custom_call_target="tpu_custom_call" | custom-call | tf_op jit(solution)/shard_map/pallas_call | solution.py:222
  33.9 0.6 %copy.10 = f32[16,512]{1,0:T(8,128)} copy(f32[16,512]{1,0:T(8,128)S(1)} %shard_map.55) | data formatting | bytes 65536
Async XLA Ops:
  0.0 2.4 %copy-start = (f32[512,512]{1,0:T(8,128)S(1)}, f32[512,512]{1,0:T(8,128)}, u32[]{:S(2)}) copy-start(f32[512,512]{1,0:T(8,128)} %propagator_ref.1) | copy-start | bytes 3145732
  1.1 1.3 %copy-start.1 = (f32[256,512]{1,0:T(8,128)S(1)}, f32[256,512]{1,0:T(8,128)}, u32[]{:S(2)}) copy-start(f32[256,512]{1,0:T(8,128)} %coefficients_ref.1) | copy-start | bytes 1572868
  1.1 1.3 %copy-start.2 = (f32[3,256]{1,0:T(4,128)S(1)}, f32[3,256]{1,0:T(4,128)}, u32[]{:S(2)}) copy-start(f32[3,256]{1,0:T(4,128)} %velocity_ref.1) | copy-start | bytes 9220

commit v3 on v2

--- a/solution.py
+++ b/solution.py
@@ -9,7 +9,6 @@
 from jax.sharding import PartitionSpec as P
 
 ITERS = 2
-WIRE = jnp.bfloat16
 PAD = 8
 
 step_size = 4.0
@@ -33,18 +32,26 @@
 
 def kernel(
     sizes, wide, narrow, scale,
-    basis_ref, kappa_ref, velocity_ref, coefficients_ref, propagator_ref, out_ref,
-    faces, halo_x, halo_y, field, forcing_ref, turned, g_high, g_low,
-    pair_out, pair_in, reduced, kept, landed, gathered,
-    halo_send, halo_recv, pair_send, pair_recv, r_send, r_recv, g_send, g_recv, f_send, f_recv,
+    basis_hbm, kappa_ref, velocity_ref, coefficients_hbm, propagator_hbm, out_ref,
+    raw, coefficients_ref, propagator_ref, basis_ref, kappa_column, halo_x, halo_y, field, forcing_ref, turned, g_high, g_low,
+    pair_out, pair_in, reduced, reduced_last, kept, landed, landed_last, gathered,
+    load, halo_send, halo_recv, pair_send, pair_recv, r_send, r_recv, g_send, g_recv, f_send, f_recv,
 ):
     size_x, size_y, size_z = sizes
     rows = size_y * size_z
     samples, modes = coefficients_ref.shape
+    cells, side = size_x * rows, size_x * size_z
     owned = samples // (wide * narrow)
     chunk = owned * narrow
     me_w, me_n = lax.axis_index("wide"), lax.axis_index("narrow")
 
+    loads = [
+        pltpu.make_async_copy(basis_hbm, raw, load.at[0]),
+        pltpu.make_async_copy(coefficients_hbm, coefficients_ref, load.at[1]),
+        pltpu.make_async_copy(propagator_hbm, propagator_ref, load.at[2]),
+    ]
+    for copy in loads:
+        copy.start()
     halo_x[...] = jnp.zeros_like(halo_x)
     halo_y[...] = jnp.zeros_like(halo_y)
     barrier = pltpu.get_barrier_semaphore()
@@ -55,13 +62,7 @@
             device_id_type=pl.DeviceIdType.MESH,
         )
 
-    for x in range(size_x):
-        at = x * rows
-        faces[0, x * size_z:(x + 1) * size_z, :] = basis_ref[at:at + size_z, :]
-        faces[1, x * size_z:(x + 1) * size_z, :] = basis_ref[at + rows - size_z:at + rows, :]
-    g_high[...] = propagator_ref[...].astype(jnp.bfloat16)
-    g_low[...] = (propagator_ref[...] - g_high[...].astype(jnp.float32)).astype(jnp.bfloat16)
-
+    loads[0].wait()
     pl.semaphore_wait(barrier, len(greeted))
 
     def remote(src, dst, send, recv, **where):
@@ -70,19 +71,29 @@
             device_id=where, device_id_type=pl.DeviceIdType.MESH,
         )
 
-    last = (size_x - 1) * rows
     halos = (
-        (remote(faces.at[1], halo_y.at[0], halo_send.at[0], halo_recv.at[0], narrow=lax.rem(me_n + 1, narrow)),
+        (remote(raw.at[size_x - 1], halo_x.at[0], halo_send.at[2], halo_recv.at[2], wide=lax.rem(me_w + 1, wide)),
+         me_w < wide - 1, me_w > 0),
+        (remote(raw.at[0], halo_x.at[1], halo_send.at[3], halo_recv.at[3], wide=lax.rem(me_w + wide - 1, wide)),
+         me_w > 0, me_w < wide - 1),
+        (remote(raw.at[:, size_y - 1], halo_y.at[0], halo_send.at[0], halo_recv.at[0], narrow=lax.rem(me_n + 1, narrow)),
          me_n < narrow - 1, me_n > 0),
-        (remote(faces.at[0], halo_y.at[1], halo_send.at[1], halo_recv.at[1], narrow=lax.rem(me_n + narrow - 1, narrow)),
+        (remote(raw.at[:, 0], halo_y.at[1], halo_send.at[1], halo_recv.at[1], narrow=lax.rem(me_n + narrow - 1, narrow)),
          me_n > 0, me_n < narrow - 1),
-        (remote(basis_ref.at[pl.ds(last, rows)], halo_x.at[0], halo_send.at[2], halo_recv.at[2], wide=lax.rem(me_w + 1, wide)),
-         me_w < wide - 1, me_w > 0),
-        (remote(basis_ref.at[pl.ds(0, rows)], halo_x.at[1], halo_send.at[3], halo_recv.at[3], wide=lax.rem(me_w + wide - 1, wide)),
-         me_w > 0, me_w < wide - 1),
     )
     for copy, sends, receives in halos:
         pl.when(sends)(copy.start)
+
+    for x in range(size_x):
+        basis_ref[x * rows:(x + 1) * rows, :] = raw[x].reshape(rows, modes)
+    row = lax.broadcasted_iota(jnp.int32, (rows, size_y), 0)
+    lane = lax.broadcasted_iota(jnp.int32, (rows, size_y), 1)
+    for x in range(size_x):
+        picked = jnp.zeros((rows, size_y), jnp.float32)
+        for z in range(size_z):
+            picked = jnp.where(row == lane * size_z + z, kappa_ref[x, z:z + 1, :], picked)
+        kappa_column[x * rows:(x + 1) * rows, :] = jnp.sum(picked, axis=1, keepdims=True)
+    loads[1].wait()
 
     z_index = lax.broadcasted_iota(jnp.int32, (rows, samples), 0) % size_z
     first_row = (me_w * narrow + me_n) * owned
@@ -96,13 +107,23 @@
         return dot(of, lift_rows, NT).astype(jnp.bfloat16).astype(jnp.float32)
 
     for step in range(ITERS):
-        field[1:size_x + 1, PAD:PAD + rows, :] = lifted(basis_ref[...]).reshape(size_x, rows, samples)
         if step == 0:
+            inner = lifted(basis_ref[0:cells, :])
             for copy, sends, receives in halos:
                 pl.when(receives)(copy.wait_recv)
-        field[0, PAD:PAD + rows, :] = lifted(halo_x[0])
-        field[size_x + 1, PAD:PAD + rows, :] = lifted(halo_x[1])
-        before, after = lifted(halo_y[0]), lifted(halo_y[1])
+            for k in range(2):
+                at = cells + k * rows
+                basis_ref[at:at + rows, :] = halo_x[k].reshape(rows, modes)
+                at = cells + 2 * rows + k * side
+                basis_ref[at:at + side, :] = halo_y[k].reshape(side, modes)
+            outer = lifted(basis_ref[cells:, :])
+        else:
+            both = lifted(basis_ref[...])
+            inner, outer = both[:cells], both[cells:]
+        field[1:size_x + 1, PAD:PAD + rows, :] = inner.reshape(size_x, rows, samples)
+        field[0, PAD:PAD + rows, :] = outer[:rows]
+        field[size_x + 1, PAD:PAD + rows, :] = outer[rows:2 * rows]
+        before, after = outer[2 * rows:2 * rows + side], outer[2 * rows + side:]
         for x in range(size_x):
             field[x + 1, PAD - size_z:PAD, :] = before[x * size_z:(x + 1) * size_z]
             field[x + 1, PAD + rows:PAD + rows + size_z, :] = after[x * size_z:(x + 1) * size_z]
@@ -120,7 +141,7 @@
             carried = carried + velocity_ref[1:2, :] * (y_next * y_next - y_prev * y_prev)
             carried = carried + velocity_ref[2:3, :] * (z_next * z_next - z_prev * z_prev)
             at = pl.multiple_of(x * rows, rows)
-            result = kappa_ref[pl.ds(at, rows), :] * spread - 0.25 * carried
+            result = kappa_column[pl.ds(at, rows), :] * spread - 0.25 * carried
             forcing_ref[pl.ds(at, rows), :] = result.astype(jnp.bfloat16)
             return carry
 
@@ -129,8 +150,11 @@
 
         def projected(target):
             at = pl.multiple_of(target * chunk, chunk)
-            return dot(turned[pl.ds(at, chunk), :], basis_ref[...], NN)
-
+            return dot(turned[pl.ds(at, chunk), :], basis_ref[0:cells, :], NN)
+
+        final = step + 1 == ITERS
+        ready = reduced_last if final else reduced.at[step]
+        arrived = landed_last if final else landed.at[step]
         pairs = []
         for i in reversed(range(wide // 2)):
             pair_out[step, i] = projected(peer(me_w, 2 * i + 1))
@@ -148,24 +172,28 @@
             total = total + pair_in[step, i]
             for n in range(narrow):
                 block = total[n * owned:(n + 1) * owned]
-                reduced[step, i, n] = block.astype(WIRE)
+                ready[i, n] = block.astype(ready.dtype)
                 if i == 0:
                     kept[n] = block
             for d in reversed(range(narrow)):
                 if i == 0 and d == 0:
                     continue
                 copy = remote(
-                    reduced.at[step, i, peer(me_n, d)], landed.at[step, i, d],
+                    ready.at[i, peer(me_n, d)], arrived.at[i, d],
                     r_send.at[step, i, d], r_recv.at[step, i, d],
                     wide=peer(me_w, 2 * i), narrow=peer(me_n, d),
                 )
                 copy.start()
                 spread_out.append((i, d, copy))
+        if step == 0:
+            loads[2].wait()
+            g_high[...] = propagator_ref[...].astype(jnp.bfloat16)
+            g_low[...] = (propagator_ref[...] - g_high[...].astype(jnp.float32)).astype(jnp.bfloat16)
         summed = kept[me_n]
         for i, d, copy in reversed(spread_out):
             copy.wait_recv()
             pending.append(copy)
-            summed = summed + landed[step, i, d].astype(jnp.float32)
+            summed = summed + arrived[i, d].astype(jnp.float32)
 
         update = state + step_size * (summed * scale)
         high = update.astype(jnp.bfloat16)
@@ -219,15 +247,20 @@
     f32, bf16 = jnp.float32, jnp.bfloat16
     dma = pltpu.SemaphoreType.DMA
     vmem = pl.BlockSpec(memory_space=pltpu.VMEM)
+    hbm = pl.BlockSpec(memory_space=pltpu.HBM)
     return pl.pallas_call(
         functools.partial(kernel, (size_x, size_y, size_z), wide, narrow, scale),
         out_shape=jax.ShapeDtypeStruct((owned, modes), f32),
-        in_specs=[vmem] * 5,
+        in_specs=[hbm, vmem, vmem, hbm, hbm],
         out_specs=vmem,
         scratch_shapes=[
-            pltpu.VMEM((2, size_x * size_z, modes), bf16),
-            pltpu.VMEM((2, rows, modes), bf16),
-            pltpu.VMEM((2, size_x * size_z, modes), bf16),
+            pltpu.VMEM((size_x, size_y, size_z, modes), bf16),
+            pltpu.VMEM((samples, modes), f32),
+            pltpu.VMEM((modes, modes), f32),
+            pltpu.VMEM((cells + 2 * (size_x + size_y) * size_z, modes), bf16),
+            pltpu.VMEM((cells, 1), f32),
+            pltpu.VMEM((2, size_y, size_z, modes), bf16),
+            pltpu.VMEM((2, size_x, size_z, modes), bf16),
             pltpu.VMEM((size_x + 2, rows + 2 * PAD, samples), f32),
             pltpu.VMEM((cells, samples), bf16),
             pltpu.VMEM((samples, cells), bf16),
@@ -235,20 +268,22 @@
             pltpu.VMEM((modes, modes), bf16),
             pltpu.VMEM((ITERS, wide // 2, chunk, modes), f32),
             pltpu.VMEM((ITERS, wide // 2, chunk, modes), f32),
-            pltpu.VMEM((ITERS, wide // 2, narrow, owned, modes), WIRE),
+            pltpu.VMEM((ITERS - 1, wide // 2, narrow, owned, modes), f32),
+            pltpu.VMEM((wide // 2, narrow, owned, modes), bf16),
             pltpu.VMEM((narrow, owned, modes), f32),
-            pltpu.VMEM((ITERS, wide // 2, narrow, owned, modes), WIRE),
+            pltpu.VMEM((ITERS - 1, wide // 2, narrow, owned, modes), f32),
+            pltpu.VMEM((wide // 2, narrow, owned, modes), bf16),
             pltpu.VMEM((ITERS - 1, wide, narrow, owned, modes), bf16),
-            dma((4,)), dma((4,)),
+            dma((3,)), dma((4,)), dma((4,)),
             dma((ITERS, wide // 2)), dma((ITERS, wide // 2)),
             dma((ITERS, wide // 2, narrow)), dma((ITERS, wide // 2, narrow)),
             dma((ITERS - 1, wide // 2, narrow)), dma((ITERS - 1, wide // 2, narrow)),
             dma((ITERS - 1, wide // 2, narrow)), dma((ITERS - 1, wide // 2, narrow)),
         ],
         compiler_params=pltpu.CompilerParams(
-            collective_id=0, has_side_effects=True, vmem_limit_bytes=48 * 1024 * 1024
+            collective_id=0, has_side_effects=True, vmem_limit_bytes=60 * 1024 * 1024
         ),
-    )(basis.reshape(cells, modes), kappa.reshape(cells, 1), velocity, coefficients, propagator)
+    )(basis, kappa.transpose(0, 2, 1), velocity, coefficients, propagator)
 
 
 def solution(mesh):

time: 34.7 us -> 37.2 us (1.072)
  Pallas kernels: 31.4 us -> 35.6 us
  local copies, waits for them, and re-layouts: 3 us -> 1.38 us
    pallas_call x1, Pallas kernels: 31.4 us -> 35.6 us  [body(): pl.pallas_call(functools.partial(kernel, (size_x, size_y, size_z), wide,...]
    reshape x2 -> x0, local copies, waits for them, and re-layouts: 1.39 us -> none  [the longest x1 1.3 us: body(): basis.reshape(cells, modes)]
    unnamed x8 -> x1, local copies, waits for them, and re-layouts: 1.6 us -> 1.38 us
where the time goes in v3:
time: 37.2 us; the launch traced here: 37 us
  Pallas kernels  35.6 us (96%)
  local copies, waits for them, and re-layouts  1.38 us (4%)
    pallas_call x1, Pallas kernels, body(): pl.pallas_call(functools.partial(kernel, (size_x, size_y, size_z), wide,...  35.6 us
    unnamed x1, local copies, waits for them, and re-layouts  1.38 us

profile of v3, /device:TPU:0, one launch (start us, length us, event | category | flops | bytes accessed | tf_op | source)
XLA Modules:
  0.0 37.0 jit_solution(18260291118386649278)
XLA Ops:
  0.0 35.6 %shard_map.55 = f32[16,512]{1,0:T(8,128)} custom-call(bf16[16,16,2,512]{3,2,1,0:T(2,128)(2,1)} %basis_hbm.1, f32[16,2,16]{2,1,0:T(2,128)} %bitcast.1, f32[3,256]{1,0:T(4,128)} %velocity_ref.1, f32[256,512]{1,0:T(8,128)} %coefficients_hbm.1, f32[512,512]{1,0:T(8,128)} %propagator_hbm.1), custom_call_target="tpu_custom_call" | custom-call | tf_op jit(solution)/shard_map/pallas_call | solution.py:251
  35.6 1.4 %copy.7 = f32[16,512]{1,0:T(8,128)} copy(f32[16,512]{1,0:T(8,128)} %shard_map.55) | data formatting | bytes 65536
